TPU v7x, 512 devices: a whole 4x8x8 slice. The times are simulated.
512 devices in a mesh: ep: 128 (over y, z, core), rep: 4 (over x).
Axes of the slice: x: 4, y: 8, z: 8, core: 2. Of those that a mesh axis runs over, the one named last changes fastest.
Arguments:
- tokens: bfloat16 [2048, 3584], P('ep', 'rep'), may hold values from -6 to 6
- expert_ids: int32 [2048, 8], P('ep'), may hold values from 0 to 127, all different within a row; in each aligned block of 16 rows (0 to 15, 16 to 31, ...) at most 2 rows name the same one
- gate_weights: float32 [2048, 8], P('ep'), may hold values from 0.05 to 0.5
- up_weight: bfloat16 [128, 3584, 1024], P('ep', 'rep'), may hold values from -0.09375 to 0.09375
- down_weight: bfloat16 [128, 1024, 3584], P('ep', None, 'rep'), may hold values from -0.1875 to 0.1875
Outputs:
- mixture: bfloat16 [2048, 3584], P('ep', 'rep')
Inputs may be any that keep to these rules, and one draw needn't show every extreme that they name: `expert_ids`: the 8 experts of a token differ. Within the rows of one device (each aligned block of 16 tokens) no expert is named by more than 2 tokens, a bound that some block reaches.
All inputs are finite; a program needn't handle non-finite values.
Results may differ from a plain program's by a relative error of at most 0.017.
Values may be sent and summed in bfloat16 or wider, within the bound.
A program may use at most 64 MiB of HBM per device.

v0:
```python
import jax
import jax.numpy as jnp
from jax import lax
from jax.sharding import PartitionSpec as P


def local(tokens, expert_ids, gate_weights, up_weight, down_weight):
    n_peers = lax.axis_size("ep")
    tok_rows, top_count = expert_ids.shape
    width_part = tokens.shape[1]
    capacity = min(tok_rows, max(2, 3 * tok_rows * top_count // (2 * n_peers)))
    flat_ids = expert_ids.reshape(-1)
    onehot = (flat_ids[:, None] == jnp.arange(n_peers, dtype=jnp.int32)[None, :]).astype(jnp.int32)
    before = jnp.cumsum(onehot, axis=0) - onehot
    ranking = jnp.sum(before * onehot, axis=1)
    slot_index = flat_ids * capacity + ranking
    token_of_row = jnp.arange(tok_rows * top_count, dtype=jnp.int32) // top_count
    outbound = (
        jnp.zeros((n_peers * capacity, width_part), tokens.dtype)
        .at[slot_index]
        .set(tokens[token_of_row])
    )
    inbound = lax.all_to_all(outbound, "ep", split_axis=0, concat_axis=0, tiled=True)
    up_local = up_weight[0]
    down_local = down_weight[0]
    partial_pre = jnp.dot(inbound, up_local, preferred_element_type=jnp.float32)
    pre_total = lax.psum(partial_pre.astype(jnp.bfloat16), "rep").astype(jnp.float32)
    hidden = jax.nn.silu(pre_total).astype(jnp.bfloat16)
    expert_out = jnp.dot(hidden, down_local, preferred_element_type=jnp.float32).astype(
        jnp.bfloat16
    )
    returned = lax.all_to_all(expert_out, "ep", split_axis=0, concat_axis=0, tiled=True)
    picked = returned[slot_index].astype(jnp.float32).reshape(tok_rows, top_count, width_part)
    mixture = jnp.sum(gate_weights[:, :, None] * picked, axis=1)
    return mixture.astype(jnp.bfloat16)


def solution(mesh):
    placed = (
        P("ep", "rep"),
        P("ep", None),
        P("ep", None),
        P("ep", "rep", None),
        P("ep", None, "rep"),
    )
    return jax.shard_map(
        local, mesh=mesh, in_specs=placed, out_specs=P("ep", "rep"), check_vma=False
    )
```

profile of v0, /device:TPU:1, one launch (start us, length us, event | category | flops | bytes accessed | tf_op | source)
XLA Modules:
  0.0 142.5 jit_solution(13055652494298791884)
XLA Ops:
  6.5 0.0 copy-start
  6.5 0.0 all-reduce.2.cloned.1.call-start
  6.5 0.9 copy.11
  7.4 0.7 broadcast_multiply_fusion
  8.1 0.1 eq.15
  8.2 0.1 fusion.20
  8.3 0.2 reduce_window_sum.11
  8.5 0.2 select_reduce_fusion
  8.7 0.1 copy.10
  8.7 0.1 mul.34
  8.9 3.2 %scatter_custom_fusion = bf16[256,896]{1,0:T(8,128)(2,1)S(1)} fusion(s32[128]{0:T(128)S(1)} %fusion.22, bf16[16,896]{1,0:T(8,128)(2,1)} %param.5, s32[1024]{0:T(1024)S(1)} %pad_clamp_fusion.1, bf16[]{:T(256)} %constant.26.clone.1), kind=kCustom, calls=%fused_computation.18 | custom fusion | bytes 459264 | tf_op jit(solution)/shard_map/scatter | solution.py:21
  12.1 0.2 all_to_all.16
  12.3 36.4 %all_to_all.24 = bf16[128,2,896]{2,1,0:T(2,128)(2,1)S(1)} all-to-all(bf16[128,2,896]{2,1,0:T(2,128)(2,1)S(1)} %all_to_all.16), channel_id=1, replica_groups=mesh['ep'=128,'rep'=4] {'ep'}, dimensions={0} | all-to-all | bytes 917504 | tf_op jit(solution)/shard_map/all_to_all | solution.py:23
  48.7 0.2 all_to_all.18
  48.9 0.0 copy-done
  48.9 1.6 %fusion.4 = bf16[256,1024]{1,0:T(8,128)(2,1)} fusion(bf16[256,896]{1,0:T(8,128)(2,1)S(1)} %all_to_all.18, bf16[1,896,1024]{2,1,0:T(8,128)(2,1)S(1)} %copy-done), kind=kOutput, calls=%fused_computation.9 | convolution fusion | flops 470024192 | bytes 2818048 | tf_op jit(solution)/shard_map/dot_general | solution.py:26
  50.5 0.0 all-reduce.2.cloned.1.call-update
  50.5 45.2 %all-reduce.2.cloned.1.call-done = bf16[256,1024]{1,0:T(8,128)(2,1)} async-done(((bf16[256,1024]{1,0:T(8,128)(2,1)}), bf16[256,1024]{1,0:T(8,128)(2,1)}) %all-reduce.2.cloned.1.call-update) | async-done | bytes 524304 | tf_op jit(solution)/shard_map/psum | solution.py:27
  95.7 2.4 %fusion.7 = bf16[256,896]{1,0:T(8,128)(2,1)S(1)} fusion(bf16[1,1024,896]{2,1,0:T(8,128)(2,1)} %param.9, bf16[256,1024]{1,0:T(8,128)(2,1)} %all-reduce.2.cloned.1.call-done), kind=kOutput, calls=%fused_computation.10 | convolution fusion | flops 471564288 | bytes 2818048 | tf_op jit(solution)/shard_map/dot_general | solution.py:29
  98.1 0.0 copy-start.1
  98.1 0.9 all_to_all.19
  99.0 16.5 %all-to-all-start.1 = ((bf16[128,2,896]{2,1,0:T(2,128)(2,1)}), bf16[128,2,896]{2,1,0:T(2,128)(2,1)S(1)}, u32[]{:S(2)}, u32[]{:S(2)}) async-start(bf16[128,2,896]{2,1,0:T(2,128)(2,1)} %all_to_all.19), calls=%async_computation.1 | async-start | bytes 917504 | tf_op jit(solution)/shard_map/all_to_all | solution.py:32
  115.5 0.0 copy-done.1
  115.5 0.1 copy.9
  115.6 18.1 %all-to-all-done.1 = bf16[128,2,896]{2,1,0:T(2,128)(2,1)S(1)} async-done(((bf16[128,2,896]{2,1,0:T(2,128)(2,1)}), bf16[128,2,896]{2,1,0:T(2,128)(2,1)S(1)}, u32[]{:S(2)}, u32[]{:S(2)}) %all-to-all-start.1) | async-done | bytes 458784 | tf_op jit(solution)/shard_map/all_to_all | solution.py:32
  133.7 0.2 all_to_all.21
  133.9 0.9 gather_fusion
  134.8 0.8 fusion.16
  (4 shorter events, 0.0 us)
Async XLA Ops:
  6.5 42.3 %copy-start = (bf16[1,896,1024]{2,1,0:T(8,128)(2,1)S(1)}, bf16[1,896,1024]{2,1,0:T(8,128)(2,1)}, u32[]{:S(2)}) copy-start(bf16[1,896,1024]{2,1,0:T(8,128)(2,1)} %param.8) | copy-start | bytes 5505028
  6.5 89.1 %all-reduce.2.cloned.1.call-start = ((), (), s32[]{:S(2)}) async-start(), calls=%async_computation.2 | async-start | bytes 1048576 | tf_op jit(solution)/shard_map/psum | solution.py:27
  98.1 17.4 %copy-start.1 = (f32[16,8]{0,1:T(8,128)S(1)}, f32[16,8]{0,1:T(8,128)}, u32[]{:S(2)}) copy-start(f32[16,8]{0,1:T(8,128)} %param.7) | copy-start | bytes 1540
  99.0 34.7 %all-to-all-start.1 = ((bf16[128,2,896]{2,1,0:T(2,128)(2,1)}), bf16[128,2,896]{2,1,0:T(2,128)(2,1)S(1)}, u32[]{:S(2)}, u32[]{:S(2)}) async-start(bf16[128,2,896]{2,1,0:T(2,128)(2,1)} %all_to_all.19), calls=%async_computation.1 | async-start | bytes 917504 | tf_op jit(solution)/shard_map/all_to_all | solution.py:32
Sparse Core Ops, SparseCore 0:
  50.6 45.0 all-reduce.1
where the time goes:
time: 143 us; the launch traced here: 142 us
  waiting for transfers between devices  63.3 us (44%)
  blocking collectives  36.4 us (25%)
  starting transfers between devices  16.5 us (12%)
  between operations  13.5 us (9%)
  local copies, waits for them, and re-layouts  6.8 us (5%)
  matrix products  3.98 us (3%)
  other arithmetic  1.96 us (1%)
    psum x1, waiting for transfers between devices, local(): lax.psum(partial_pre.astype(jnp.bfloat16), 'rep').astype(jnp.float32)  45.2 us
    all_to_all x1, blocking collectives, local(): lax.all_to_all(outbound, 'ep', split_axis=0, concat_axis=0, tiled=True)  36.4 us
    all_to_all x1, waiting for transfers between devices, local(): lax.all_to_all(expert_out, 'ep', split_axis=0, concat_axis=0, tiled=True)  18.1 us
    all_to_all x1, starting transfers between devices, local(): lax.all_to_all(expert_out, 'ep', split_axis=0, concat_axis=0, tiled=True)  16.5 us
    scatter x1, local copies, waits for them, and re-layouts, local(): outbound = jnp.zeros((n_peers * capacity, width_part), tokens.dtype).at[s...  3.23 us
  transfers between devices with their start and end apart: 2, of which 2 were waited for; matrix products, arithmetic and copies ran while one was open for 0% of the time, Pallas kernels for 0%

commit v1 on v0

--- a/solution.py
+++ b/solution.py
@@ -24,7 +24,9 @@
     up_local = up_weight[0]
     down_local = down_weight[0]
     partial_pre = jnp.dot(inbound, up_local, preferred_element_type=jnp.float32)
-    pre_total = lax.psum(partial_pre.astype(jnp.bfloat16), "rep").astype(jnp.float32)
+    pre_total = jnp.sum(lax.all_gather(partial_pre.astype(jnp.bfloat16), "rep"), axis=0).astype(
+        jnp.float32
+    )
     hidden = jax.nn.silu(pre_total).astype(jnp.bfloat16)
     expert_out = jnp.dot(hidden, down_local, preferred_element_type=jnp.float32).astype(
         jnp.bfloat16

time: 143 us -> 127 us (0.89)
  waiting for transfers between devices: 63.3 us -> 47.6 us
  starting transfers between devices: 16.5 us -> 14.4 us
  other arithmetic: 1.96 us -> 3.99 us
    psum x1 -> x0, waiting for transfers between devices: 45.2 us -> none  [local(): lax.psum(partial_pre.astype(jnp.bfloat16), 'rep').astype(jnp.float32)]
    all_gather x0 -> x1, waiting for transfers between devices: none -> 29.5 us  [local(): lax.all_gather(partial_pre.astype(jnp.bfloat16), 'rep')]
    all_to_all x1, starting transfers between devices: 16.5 us -> 14.4 us  [local(): lax.all_to_all(expert_out, 'ep', split_axis=0, concat_axis=0, tiled=True)]
    reduce_sum x0 -> x1, other arithmetic: none -> 2.02 us  [local(): jnp.sum(lax.all_gather(partial_pre.astype(jnp.bfloat16), 'rep'), axis=0)]
where the time goes in v1:
time: 127 us
  waiting for transfers between devices  47.6 us (37%)
  blocking collectives  36.4 us (29%)
  starting transfers between devices  14.4 us (11%)
  between operations  13.5 us (11%)
  local copies, waits for them, and re-layouts  7.08 us (6%)
  other arithmetic  3.99 us (3%)
  matrix products  3.84 us (3%)
    all_to_all x1, blocking collectives, local(): lax.all_to_all(outbound, 'ep', split_axis=0, concat_axis=0, tiled=True)  36.4 us
    all_gather x1, waiting for transfers between devices, local(): lax.all_gather(partial_pre.astype(jnp.bfloat16), 'rep')  29.5 us
    all_to_all x1, waiting for transfers between devices, local(): lax.all_to_all(expert_out, 'ep', split_axis=0, concat_axis=0, tiled=True)  18.1 us
    all_to_all x1, starting transfers between devices, local(): lax.all_to_all(expert_out, 'ep', split_axis=0, concat_axis=0, tiled=True)  14.4 us
    scatter x1, local copies, waits for them, and re-layouts, local(): outbound = jnp.zeros((n_peers * capacity, width_part), tokens.dtype).at[s...  3.51 us
  transfers between devices with their start and end apart: 2, of which 2 were waited for; matrix products, arithmetic and copies ran while one was open for 0% of the time, Pallas kernels for 0%

profile of v1, /device:TPU:1, one launch (start us, length us, event | category | flops | bytes accessed | tf_op | source)
XLA Modules:
  0.0 126.9 jit_solution(14805645848831851307)
XLA Ops:
  6.5 0.0 copy-start
  6.5 0.0 all-gather.3.cloned.1.call-start
  6.5 0.9 copy.11
  7.4 0.7 broadcast_multiply_fusion
  8.1 0.1 eq.15
  8.2 0.1 fusion.20
  8.3 0.2 reduce_window_sum.11
  8.5 0.2 select_reduce_fusion
  8.7 0.1 copy.10
  8.7 0.1 mul.34
  8.9 3.5 %scatter_custom_fusion = bf16[256,896]{1,0:T(8,128)(2,1)S(1)} fusion(s32[128]{0:T(128)S(1)} %fusion.22, bf16[16,896]{1,0:T(8,128)(2,1)} %param.5, s32[1024]{0:T(1024)S(1)} %pad_clamp_fusion.1, bf16[]{:T(256)} %constant.27.clone.1), kind=kCustom, calls=%fused_computation.18 | custom fusion | bytes 459264 | tf_op jit(solution)/shard_map/scatter | solution.py:21
  12.4 0.2 all_to_all.16
  12.6 36.4 %all_to_all.24 = bf16[128,2,896]{2,1,0:T(2,128)(2,1)S(1)} all-to-all(bf16[128,2,896]{2,1,0:T(2,128)(2,1)S(1)} %all_to_all.16), channel_id=1, replica_groups=mesh['ep'=128,'rep'=4] {'ep'}, dimensions={0} | all-to-all | bytes 917504 | tf_op jit(solution)/shard_map/all_to_all | solution.py:23
  49.0 0.2 all_to_all.18
  49.2 0.0 copy-done
  49.2 1.5 %fusion.4 = bf16[256,1024]{1,0:T(8,128)(2,1)} fusion(bf16[256,896]{1,0:T(8,128)(2,1)S(1)} %all_to_all.18, bf16[1,896,1024]{2,1,0:T(8,128)(2,1)S(1)} %copy-done), kind=kOutput, calls=%fused_computation.9 | convolution fusion | flops 470024192 | bytes 2818048 | tf_op jit(solution)/shard_map/dot_general | solution.py:26
  50.7 0.0 all-gather.3.cloned.1.call-update
  50.7 29.5 %all-gather.3.cloned.1.call-done = bf16[1024,1024]{1,0:T(8,128)(2,1)} async-done(((bf16[256,1024]{1,0:T(8,128)(2,1)}), bf16[1024,1024]{1,0:T(8,128)(2,1)}) %all-gather.3.cloned.1.call-update) | async-done | bytes 2097168 | tf_op jit(solution)/shard_map/all_gather | solution.py:27
  80.2 2.0 %reduce_sum.34 = bf16[256,1024]{1,0:T(8,128)(2,1)S(1)} reduce(bf16[4,256,1024]{2,1,0:T(8,128)(2,1)} %bitcast.23, bf16[]{:T(256)} %constant.27.clone.1), dimensions={0}, to_apply=%region_3.4 | reduce | flops 786432 | bytes 2621442 | tf_op jit(solution)/shard_map/reduce_sum | solution.py:27
  82.3 2.3 %fusion.7 = bf16[256,896]{1,0:T(8,128)(2,1)S(1)} fusion(bf16[1,1024,896]{2,1,0:T(8,128)(2,1)} %param.9, bf16[256,1024]{1,0:T(8,128)(2,1)S(1)} %reduce_sum.34), kind=kOutput, calls=%fused_computation.10 | convolution fusion | flops 471564288 | bytes 2818048 | tf_op jit(solution)/shard_map/dot_general | solution.py:31
  84.6 0.0 copy-start.1
  84.6 0.9 all_to_all.19
  85.5 14.4 %all-to-all-start.1 = ((bf16[128,2,896]{2,1,0:T(2,128)(2,1)}), bf16[128,2,896]{2,1,0:T(2,128)(2,1)S(1)}, u32[]{:S(2)}, u32[]{:S(2)}) async-start(bf16[128,2,896]{2,1,0:T(2,128)(2,1)} %all_to_all.19), calls=%async_computation.1 | async-start | bytes 917504 | tf_op jit(solution)/shard_map/all_to_all | solution.py:34
  100.0 0.0 copy-done.1
  100.0 0.1 copy.9
  100.0 18.1 %all-to-all-done.1 = bf16[128,2,896]{2,1,0:T(2,128)(2,1)S(1)} async-done(((bf16[128,2,896]{2,1,0:T(2,128)(2,1)}), bf16[128,2,896]{2,1,0:T(2,128)(2,1)S(1)}, u32[]{:S(2)}, u32[]{:S(2)}) %all-to-all-start.1) | async-done | bytes 458784 | tf_op jit(solution)/shard_map/all_to_all | solution.py:34
  118.2 0.2 all_to_all.21
  118.4 0.9 gather_fusion
  119.2 0.8 fusion.16
  (4 shorter events, 0.0 us)
Async XLA Ops:
  6.5 42.6 %copy-start = (bf16[1,896,1024]{2,1,0:T(8,128)(2,1)S(1)}, bf16[1,896,1024]{2,1,0:T(8,128)(2,1)}, u32[]{:S(2)}) copy-start(bf16[1,896,1024]{2,1,0:T(8,128)(2,1)} %param.8) | copy-start | bytes 5505028
  6.5 73.7 %all-gather.3.cloned.1.call-start = ((), (), s32[]{:S(2)}) async-start(), calls=%async_computation.2 | async-start | bytes 2621440 | tf_op jit(solution)/shard_map/all_gather | solution.py:27
  84.6 15.4 %copy-start.1 = (f32[16,8]{0,1:T(8,128)S(1)}, f32[16,8]{0,1:T(8,128)}, u32[]{:S(2)}) copy-start(f32[16,8]{0,1:T(8,128)} %param.7) | copy-start | bytes 1540
  85.5 32.7 %all-to-all-start.1 = ((bf16[128,2,896]{2,1,0:T(2,128)(2,1)}), bf16[128,2,896]{2,1,0:T(2,128)(2,1)S(1)}, u32[]{:S(2)}, u32[]{:S(2)}) async-start(bf16[128,2,896]{2,1,0:T(2,128)(2,1)} %all_to_all.19), calls=%async_computation.1 | async-start | bytes 917504 | tf_op jit(solution)/shard_map/all_to_all | solution.py:34
Sparse Core Ops, SparseCore 0:
  50.9 29.3 all-gather.2
